TPU v7x, 32 devices: a whole 2x2x4 slice. The times are simulated.
32 devices in a mesh: groups: 2 (over x), pool: 8 (over z, y), shard: 2 (over core).
Axes of the slice: x: 2, y: 2, z: 4, core: 2. Of those that a mesh axis runs over, the one named last changes fastest.
Arguments:
- tokens: bfloat16 [2, 64, 8192], P(None, ('groups', 'pool'), 'shard'), parts along dimension 1, may hold values from -6 to 6
- counts: int32 [2, 16], P(None, ('groups', 'pool')), parts along dimension 1, may hold values from 0 to 4, as said below
- gate_up: bfloat16 [8192, 2, 28672], P('shard', None, 'pool'), may hold values from -0.0625 to 0.0625
- down: bfloat16 [28672, 8192], P('pool', 'shard'), may hold values from -0.03125 to 0.03125
Outputs:
- mixed: bfloat16 [2, 64, 8192], P(None, ('groups', 'pool'), 'shard'), parts along dimension 1
There are 2 independent parts, one for each index of `groups`. A program takes and returns all parts, laid end to end along the dimension named above; an argument that names none is the same for every part. Nothing has to cross between parts.
Inputs may be any that keep to these rules, and one draw needn't show every extreme that they name: `counts`: in each micro-batch some device has 4 live rows and some has none.
All inputs are finite; a program needn't handle non-finite values.
Results may differ from a plain program's by a relative error of at most 0.005.
Values may be sent and summed in bfloat16 or wider, within the bound.
A program may use at most 256 MiB of HBM per device.

v0:
```python
import jax
import jax.numpy as jnp
from jax import lax
from jax.sharding import PartitionSpec as P


def feed_forward(own_rows, gate_up, down):
    flat_weights = gate_up.reshape(gate_up.shape[0], -1)
    local_units = gate_up.shape[2]
    partial_sums = jnp.dot(
        lax.all_gather(own_rows, "pool", axis=0, tiled=True),
        flat_weights,
        preferred_element_type=jnp.float32,
    )
    row_total = partial_sums.shape[0]
    partial_sums = partial_sums.reshape(row_total, 2, local_units)
    summed = lax.psum(partial_sums, "shard")
    hidden = (jax.nn.silu(summed[:, 0]) * summed[:, 1]).astype(jnp.bfloat16)
    returned = lax.psum_scatter(
        jnp.dot(hidden, down, preferred_element_type=jnp.float32),
        "pool",
        scatter_dimension=0,
        tiled=True,
    )
    return returned.astype(jnp.bfloat16)


def shards(tokens, counts, gate_up, down):
    capacity = tokens.shape[1]
    position = lax.broadcasted_iota(jnp.int32, (capacity, 1), 0)
    nothing = jnp.zeros((), tokens.dtype)
    live_sets = [
        jnp.where(position < counts[micro_batch, 0], tokens[micro_batch], nothing)
        for micro_batch in range(tokens.shape[0])
    ]
    combined = jnp.concatenate(live_sets, axis=0)
    result = feed_forward(combined, gate_up, down)
    stacked = result.reshape(tokens.shape[0], capacity, result.shape[1])
    return stacked


def solution(mesh):
    placed = (
        P(None, ("groups", "pool"), "shard"),
        P(None, ("groups", "pool")),
        P("shard", None, "pool"),
        P("pool", "shard"),
    )
    return jax.shard_map(
        shards,
        mesh=mesh,
        in_specs=placed,
        out_specs=P(None, ("groups", "pool"), "shard"),
        check_vma=False,
    )
```

profile of v0, /device:TPU:0, one launch (start us, length us, event | category | flops | bytes accessed | tf_op | source)
XLA Modules:
  0.0 288.1 jit_solution(295380920429154931)
XLA Ops:
  6.5 0.0 all-reduce.2.cloned.1.call-start
  6.5 39.3 %copy.6 = bf16[512,8,2,3584]{3,1,2,0:T(8,128)(2,1)} copy(bf16[512,8,2,3584]{3,2,1,0:T(2,128)(2,1)} %bitcast.30) | data formatting | bytes 117440512
  45.8 0.0 copy-start.1
  45.8 0.0 copy-start
  45.8 69.5 %copy.5 = bf16[7168,4096]{1,0:T(8,128)(2,1)} copy(bf16[7168,4096]{0,1:T(8,128)(2,1)} %bitcast.29) | data formatting | bytes 117440512 | tf_op jit(solution)/shard_map/dot_general | solution.py:10
  115.3 0.0 copy-done.1
  115.3 0.6 fusion.8
  115.9 1.3 iota_compare_fusion
  117.3 0.0 copy-done
  117.3 0.1 bitcast_select_fusion.1
  117.4 33.0 %all_gather.3 = bf16[64,4096]{1,0:T(8,128)(2,1)S(1)} all-gather(bf16[8,4096]{1,0:T(8,128)(2,1)S(1)} %pad_maximum_fusion), channel_id=1, replica_groups=mesh['groups'=2,'pool'=8,'shard'=2] {'pool'}, dimensions={0}, use_global_device_ids=true | all-gather | bytes 589824 | tf_op jit(solution)/shard_map/all_gather | solution.py:11
  150.5 25.4 %fusion.2 = f32[64,2,3584]{2,0,1:T(8,128)} fusion(bf16[2,3584,4096]{2,1,0:T(8,128)(2,1)} %bitcast.28, bf16[64,4096]{1,0:T(8,128)(2,1)S(1)} %all_gather.3), kind=kOutput, calls=%fused_computation.4 | convolution fusion | flops 3758096384 | bytes 61079552 | tf_op jit(solution)/shard_map/dot_general | solution.py:10
  175.9 0.0 all-reduce.2.cloned.1.call-update
  175.9 0.0 reduce-scatter.2.cloned.1.call-start
  176.0 22.0 %all-reduce.2.cloned.1.call-done = f32[64,2,3584]{2,0,1:T(8,128)} async-done(((f32[64,2,3584]{2,0,1:T(8,128)}), f32[64,2,3584]{2,0,1:T(8,128)}) %all-reduce.2.cloned.1.call-update) | async-done | bytes 1835024 | tf_op jit(solution)/shard_map/psum | solution.py:17
  198.0 16.1 %fusion.4 = f32[64,4096]{1,0:T(8,128)} fusion(bf16[3584,4096]{1,0:T(8,128)(2,1)} %param.7, f32[64,2,3584]{2,0,1:T(8,128)} %all-reduce.2.cloned.1.call-done), kind=kOutput, calls=%fused_computation.6 | convolution fusion | flops 1880424448 | bytes 32243712 | tf_op jit(solution)/shard_map/dot_general | solution.py:20
  214.1 0.0 reduce-scatter.2.cloned.1.call-update
  214.1 65.6 %reduce-scatter.2.cloned.1.call-done = f32[8,4096]{1,0:T(8,128)} async-done(((f32[64,4096]{1,0:T(8,128)}), f32[8,4096]{1,0:T(8,128)}) %reduce-scatter.2.cloned.1.call-update) | async-done | bytes 131088 | tf_op jit(solution)/shard_map/reduce_scatter | solution.py:19
  279.7 0.9 convert_element_type.7
  280.6 0.7 reshape.19
  (1 shorter events, 0.0 us)
Async XLA Ops:
  6.5 191.5 %all-reduce.2.cloned.1.call-start = ((), (), s32[]{:S(2)}) async-start(), calls=%async_computation.1 | async-start | bytes 3670016 | tf_op jit(solution)/shard_map/psum | solution.py:17
  45.8 69.5 %copy-start.1 = (s32[2,1]{0,1:T(1,128)S(1)}, s32[2,1]{0,1:T(1,128)}, u32[]{:S(2)}) copy-start(s32[2,1]{0,1:T(1,128)} %param.5) | copy-start | bytes 28
  45.8 71.5 %copy-start = (bf16[2,4,4096]{2,1,0:T(4,128)(2,1)S(1)}, bf16[2,4,4096]{2,1,0:T(4,128)(2,1)}, u32[]{:S(2)}) copy-start(bf16[2,4,4096]{2,1,0:T(4,128)(2,1)} %param.4) | copy-start | bytes 196612
  175.9 103.8 %reduce-scatter.2.cloned.1.call-start = ((), (), s32[]{:S(2)}) async-start(), calls=%async_computation.2 | async-start | bytes 1179648 | tf_op jit(solution)/shard_map/reduce_scatter | solution.py:19
Sparse Core Ops, SparseCore 0:
  176.0 21.9 all-reduce.1
  214.3 65.3 reduce-scatter.1
where the time goes:
time: 290 us; the launch traced here: 288 us
  local copies, waits for them, and re-layouts  110 us (38%)
  waiting for transfers between devices  87.6 us (30%)
  matrix products  41.5 us (14%)
  blocking collectives  33 us (11%)
  between operations  13.4 us (5%)
    dot_general x1, local copies, waits for them, and re-layouts, feed_forward(): jnp.dot(lax.all_gather(own_rows, 'pool', axis=0, tiled=True), flat_weight...  69.5 us
    reduce_scatter x1, waiting for transfers between devices, feed_forward(): lax.psum_scatter(jnp.dot(hidden, down, preferred_element_type=jnp.float32...  65.6 us
    unnamed x5, local copies, waits for them, and re-layouts  39.3 us
    all_gather x1, blocking collectives, feed_forward(): lax.all_gather(own_rows, 'pool', axis=0, tiled=True)  33 us
    dot_general x1, matrix products, feed_forward(): jnp.dot(lax.all_gather(own_rows, 'pool', axis=0, tiled=True), flat_weight...  25.4 us
    psum x1, waiting for transfers between devices, feed_forward(): summed = lax.psum(partial_sums, 'shard')  22 us
    dot_general x1, matrix products, feed_forward(): jnp.dot(hidden, down, preferred_element_type=jnp.float32)  16.1 us
  transfers between devices with their start and end apart: 2, of which 2 were waited for; matrix products, arithmetic and copies ran while one was open for 0% of the time, Pallas kernels for 0%

commit v1 on v0

--- a/solution.py
+++ b/solution.py
@@ -2,6 +2,11 @@
 import jax.numpy as jnp
 from jax import lax
 from jax.sharding import PartitionSpec as P
+
+
+def gather_and_add(value, name):
+    parts = lax.all_gather(value, name)
+    return jnp.sum(parts, axis=0)
 
 
 def feed_forward(own_rows, gate_up, down):
@@ -14,7 +19,7 @@
     )
     row_total = partial_sums.shape[0]
     partial_sums = partial_sums.reshape(row_total, 2, local_units)
-    summed = lax.psum(partial_sums, "shard")
+    summed = gather_and_add(partial_sums, "shard")
     hidden = (jax.nn.silu(summed[:, 0]) * summed[:, 1]).astype(jnp.bfloat16)
     returned = lax.psum_scatter(
         jnp.dot(hidden, down, preferred_element_type=jnp.float32),

time: 290 us -> 282 us (0.972)
  waiting for transfers between devices: 87.6 us -> 79.8 us
  matrix products: 41.5 us -> 38.4 us
    psum x1 -> x0, waiting for transfers between devices: 22 us -> none  [feed_forward(): summed = lax.psum(partial_sums, 'shard')]
    all_gather x0 -> x1, waiting for transfers between devices: none -> 14.1 us  [gather_and_add(): parts = lax.all_gather(value, name)]
    dot_general x1, matrix products: 16.1 us -> 13 us  [feed_forward(): jnp.dot(hidden, down, preferred_element_type=jnp.float32)]
where the time goes in v1:
time: 282 us; the launch traced here: 280 us
  local copies, waits for them, and re-layouts  110 us (39%)
  waiting for transfers between devices  79.8 us (28%)
  matrix products  38.4 us (14%)
  blocking collectives  33 us (12%)
  between operations  13.4 us (5%)
  other arithmetic  4.84 us (2%)
    dot_general x1, local copies, waits for them, and re-layouts, feed_forward(): jnp.dot(lax.all_gather(own_rows, 'pool', axis=0, tiled=True), flat_weight...  69.5 us
    reduce_scatter x1, waiting for transfers between devices, feed_forward(): lax.psum_scatter(jnp.dot(hidden, down, preferred_element_type=jnp.float32...  65.6 us
    unnamed x5, local copies, waits for them, and re-layouts  39.3 us
    all_gather x1, blocking collectives, feed_forward(): lax.all_gather(own_rows, 'pool', axis=0, tiled=True)  33 us
    dot_general x1, matrix products, feed_forward(): jnp.dot(lax.all_gather(own_rows, 'pool', axis=0, tiled=True), flat_weight...  25.4 us
    all_gather x1, waiting for transfers between devices, gather_and_add(): parts = lax.all_gather(value, name)  14.1 us
    dot_general x1, matrix products, feed_forward(): jnp.dot(hidden, down, preferred_element_type=jnp.float32)  13 us
  transfers between devices with their start and end apart: 2, of which 2 were waited for; matrix products, arithmetic and copies ran while one was open for 0% of the time, Pallas kernels for 0%

profile of v1, /device:TPU:0, one launch (start us, length us, event | category | flops | bytes accessed | tf_op | source)
XLA Modules:
  0.0 279.6 jit_solution(17432752071016515698)
XLA Ops:
  6.5 0.0 all-gather.3.cloned.1.call-start
  6.5 39.3 %copy.8 = bf16[512,8,2,3584]{3,1,2,0:T(8,128)(2,1)} copy(bf16[512,8,2,3584]{3,2,1,0:T(2,128)(2,1)} %bitcast.31) | data formatting | bytes 117440512
  45.8 0.0 copy-start.1
  45.8 0.0 copy-start
  45.8 69.5 %copy.7 = bf16[7168,4096]{1,0:T(8,128)(2,1)} copy(bf16[7168,4096]{0,1:T(8,128)(2,1)} %bitcast.30) | data formatting | bytes 117440512 | tf_op jit(solution)/shard_map/dot_general | solution.py:15
  115.3 0.0 copy-done.1
  115.3 0.6 fusion.8
  115.9 1.3 iota_compare_fusion
  117.3 0.0 copy-done
  117.3 0.1 bitcast_select_fusion.1
  117.4 33.0 %all_gather.6 = bf16[64,4096]{1,0:T(8,128)(2,1)S(1)} all-gather(bf16[8,4096]{1,0:T(8,128)(2,1)S(1)} %pad_maximum_fusion), channel_id=1, replica_groups=mesh['groups'=2,'pool'=8,'shard'=2] {'pool'}, dimensions={0}, use_global_device_ids=true | all-gather | bytes 589824 | tf_op jit(solution)/shard_map/all_gather | solution.py:16
  150.5 25.4 %fusion.2 = f32[64,2,3584]{2,0,1:T(8,128)} fusion(bf16[2,3584,4096]{2,1,0:T(8,128)(2,1)} %bitcast.29, bf16[64,4096]{1,0:T(8,128)(2,1)S(1)} %all_gather.6), kind=kOutput, calls=%fused_computation.4 | convolution fusion | flops 3758096384 | bytes 61079552 | tf_op jit(solution)/shard_map/dot_general | solution.py:15
  175.9 0.0 all-gather.3.cloned.1.call-update
  175.9 0.0 reduce-scatter.2.cloned.1.call-start
  176.0 14.1 %all-gather.3.cloned.1.call-done = f32[128,2,3584]{2,0,1:T(8,128)} async-done(((f32[64,2,3584]{2,0,1:T(8,128)}), f32[128,2,3584]{2,0,1:T(8,128)}) %all-gather.3.cloned.1.call-update) | async-done | bytes 3670032 | tf_op jit(solution)/shard_map/all_gather | solution.py:8
  190.1 2.5 reduce_sum.9
  192.5 13.0 %fusion.4 = f32[64,4096]{1,0:T(8,128)} fusion(bf16[3584,4096]{1,0:T(8,128)(2,1)} %param.7, f32[64,2,3584]{2,0,1:T(8,128)S(1)} %reduce_sum.9), kind=kOutput, calls=%fused_computation.6 | convolution fusion | flops 1880424448 | bytes 32243712 | tf_op jit(solution)/shard_map/dot_general | solution.py:25
  205.6 0.0 reduce-scatter.2.cloned.1.call-update
  205.6 65.6 %reduce-scatter.2.cloned.1.call-done = f32[8,4096]{1,0:T(8,128)} async-done(((f32[64,4096]{1,0:T(8,128)}), f32[8,4096]{1,0:T(8,128)}) %reduce-scatter.2.cloned.1.call-update) | async-done | bytes 131088 | tf_op jit(solution)/shard_map/reduce_scatter | solution.py:24
  271.2 0.9 convert_element_type.7
  272.1 0.7 reshape.22
  (1 shorter events, 0.0 us)
Async XLA Ops:
  6.5 183.5 %all-gather.3.cloned.1.call-start = ((), (), s32[]{:S(2)}) async-start(), calls=%async_computation.2 | async-start | bytes 5505024 | tf_op jit(solution)/shard_map/all_gather | solution.py:8
  45.8 69.5 %copy-start.1 = (s32[2,1]{0,1:T(1,128)S(1)}, s32[2,1]{0,1:T(1,128)}, u32[]{:S(2)}) copy-start(s32[2,1]{0,1:T(1,128)} %param.5) | copy-start | bytes 28
  45.8 71.5 %copy-start = (bf16[2,4,4096]{2,1,0:T(4,128)(2,1)S(1)}, bf16[2,4,4096]{2,1,0:T(4,128)(2,1)}, u32[]{:S(2)}) copy-start(bf16[2,4,4096]{2,1,0:T(4,128)(2,1)} %param.4) | copy-start | bytes 196612
  175.9 95.3 %reduce-scatter.2.cloned.1.call-start = ((), (), s32[]{:S(2)}) async-start(), calls=%async_computation.1 | async-start | bytes 1179648 | tf_op jit(solution)/shard_map/reduce_scatter | solution.py:24
Sparse Core Ops, SparseCore 0:
  176.0 13.9 all-gather.2
  205.7 65.4 reduce-scatter.1
